TPU v7x, 32 devices: a whole 2x2x4 slice. The times are simulated.
32 devices in a mesh: body: 4 (over z), mort: 8 (over y, x, core).
Axes of the slice: x: 2, y: 2, z: 4, core: 2. Of those that a mesh axis runs over, the one named last changes fastest.
Arguments:
- displacement: float32 [3, 64, 256, 128], P(None, 'body', 'mort'), may hold values from -6 to 6
- body_load: float32 [3, 64, 256, 128], P(None, 'body', 'mort'), may hold values from -6 to 6
- stiffness: float32 [64, 256, 128], P('body', 'mort'), may hold values from 0.5 to 4
- initial_gap: float32 [4096, 128], P(('body', 'mort')), may hold values from -6 to 6
- weights: float32 [4096, 128], P(('body', 'mort')), may hold values from 0.05 to 1
- basis_values: float32 [4096, 4, 128], P(('body', 'mort')), may hold values from 0 to 1
- point_cell: int32 [4096, 128], P(('body', 'mort')), may hold values from 0 to 511
- point_segment: int32 [4096, 128], P(('body', 'mort')), may hold values from 0 to 255
- block_owner: int32 [4096, 1], P(('body', 'mort')), may hold values from 0 to 7; in each aligned block of 128 rows (0 to 127, 128 to 255, ...) at most 64 rows name the same one
- multipliers: float32 [4, 8192], P(None, ('body', 'mort')), may hold values from 0 to 2
- block_inverse: float32 [4, 4, 8192], P(None, None, ('body', 'mort')), may hold values from -0.9 to 1
Outputs:
- body_residual: float32 [3, 64, 256, 128], P(None, 'body', 'mort')
- new_multipliers: float32 [4, 8192], P(None, ('body', 'mort'))
Inputs may be any that keep to these rules, and one draw needn't show every extreme that they name: `block_owner`: among the 128 blocks of one device each owner is named at most 64 times.
All inputs are finite; a program needn't handle non-finite values.
Results may differ from a plain program's by a relative error of at most 0.000098.
Values sent between devices are 32-bit elements; how exact they have to be, the bound alone decides.
A program may use at most 128 MiB of HBM per device.

v0:
```python
import math

import jax
import jax.numpy as jnp
from jax import lax
from jax.sharding import PartitionSpec as P

exact = lax.Precision.HIGHEST


def extended(block, sides, width):
    for axis, dim in sides:
        count = lax.axis_size(axis)
        forward = [(i, i + 1) for i in range(count - 1)]
        backward = [(target, source) for source, target in forward]
        low = lax.ppermute(
            lax.slice_in_dim(block, block.shape[dim] - width, None, axis=dim), axis, forward
        )
        high = lax.ppermute(lax.slice_in_dim(block, 0, width, axis=dim), axis, backward)
        block = jnp.concatenate([low, block, high], axis=dim)
    return block


def grouped(fn, arrays, group):
    count = arrays[0].shape[0]
    shaped = tuple((a.reshape((count // group, group) + a.shape[1:]) for a in arrays))
    return lax.map(lambda items: fn(*items), shaped)


def newton_update(integrals, multipliers, block_inverse):
    applied = jnp.sum(block_inverse * integrals[None, :, :], axis=1)
    updated = jnp.maximum(multipliers - applied, 0.0)
    return (updated, updated - multipliers)


def body(
    displacement,
    body_load,
    stiffness,
    initial_gap,
    weights,
    basis_values,
    point_cell,
    point_segment,
    block_owner,
    multipliers,
    block_inverse,
):
    cells_x = displacement.shape[1]
    cells_y = displacement.shape[2]
    blocks = initial_gap.shape[0]
    points = initial_gap.shape[1]
    segments = multipliers.shape[1]
    mort_count = lax.axis_size("mort")
    group = math.gcd(blocks, 16)
    cell_ids = jnp.arange(cells_x * cells_y, dtype=jnp.int32)
    segment_ids_all = jnp.arange(segments, dtype=jnp.int32)
    surface = displacement[2, :, :, 0].reshape(cells_x * cells_y)

    def lookup(cells):
        onehot = (cells[:, :, None] == cell_ids[None, None, :]).astype(jnp.float32)
        return jnp.einsum("gpc,c->gp", onehot, surface, precision=exact)

    point_gap = initial_gap + grouped(lookup, (point_cell,), group).reshape(blocks, points)
    integrand = weights[:, None, :] * basis_values * point_gap[:, None, :]
    owners = block_owner[:, 0]
    owner_onehot = (owners[:, None] == jnp.arange(mort_count, dtype=jnp.int32)[None, :]).astype(
        jnp.float32
    )

    def summed(segs, terms, owner_rows):
        onehot = (segs[:, :, None] == segment_ids_all[None, None, :]).astype(jnp.float32)
        return jnp.einsum("gps,gkp,go->oks", onehot, terms, owner_rows, precision=exact)

    partial_value = jnp.sum(
        grouped(summed, (point_segment, integrand, owner_onehot), group), axis=0
    )
    integrals = lax.psum_scatter(partial_value, "mort", scatter_dimension=0, tiled=True)[0]
    updated, change = newton_update(integrals, multipliers, block_inverse)
    changes = lax.all_gather(change[None], "mort", axis=0, tiled=True)
    block_changes = jnp.einsum("bo,oks->bks", owner_onehot, changes, precision=exact)

    def picked(segs, basis, table):
        onehot = (segs[:, :, None] == segment_ids_all[None, None, :]).astype(jnp.float32)
        return jnp.einsum("gps,gks,gkp->gp", onehot, table, basis, precision=exact)

    pressure = grouped(picked, (point_segment, basis_values, block_changes), group).reshape(
        blocks, points
    )

    def spread(cells, loads):
        onehot = (cells[:, :, None] == cell_ids[None, None, :]).astype(jnp.float32)
        return jnp.einsum("gpc,gp->c", onehot, loads, precision=exact)

    traction = jnp.sum(grouped(spread, (point_cell, weights * pressure), group), axis=0)
    padded = extended(displacement, (("body", 1), ("mort", 2)), 1)
    padded = jnp.pad(padded, ((0, 0), (0, 0), (0, 0), (1, 1)))
    beside = padded[:, 2:, 1:-1, 1:-1] + padded[:, :-2, 1:-1, 1:-1]
    beside = beside + padded[:, 1:-1, 2:, 1:-1] + padded[:, 1:-1, :-2, 1:-1]
    beside = beside + padded[:, 1:-1, 1:-1, 2:] + padded[:, 1:-1, 1:-1, :-2]
    stiff_force = (6.0 + stiffness)[None] * displacement - beside
    residual = body_load - stiff_force
    residual = residual.at[2, :, :, 0].add(traction.reshape(cells_x, cells_y))
    return (residual, updated)


def solution(mesh):
    return jax.shard_map(
        body,
        mesh=mesh,
        in_specs=(
            P(None, "body", "mort", None),
            P(None, "body", "mort", None),
            P("body", "mort", None),
            P(("body", "mort"), None),
            P(("body", "mort"), None),
            P(("body", "mort"), None, None),
            P(("body", "mort"), None),
            P(("body", "mort"), None),
            P(("body", "mort"), None),
            P(None, ("body", "mort")),
            P(None, None, ("body", "mort")),
        ),
        out_specs=(P(None, "body", "mort", None), P(None, ("body", "mort"))),
        check_vma=False,
    )
```

profile of v0, /device:TPU:19, one launch (start us, length us, event | category | flops | bytes accessed | tf_op | source)
XLA Modules:
  0.0 152.1 jit_solution(2052006497745772095)
XLA Ops:
  0.6 0.9 fusion.40
  1.5 3.3 %collective-permute-start.1 = (f32[3,1,32,128]{3,2,1,0:T(8,128)S(1)}, f32[3,1,32,128]{3,2,1,0:T(8,128)S(1)}, u32[]{:S(2)}, u32[]{:S(2)}) collective-permute-start(f32[3,1,32,128]{3,2,1,0:T(8,128)S(1)} %get-tuple-element.245), channel_id=1, source_target_pairs={{0,8},{8,16},{16,24},{1,9},{9,17},{17,25},{2,10},{10,18},{18,26},{... | collective-permute-start | bytes 147464 | tf_op jit(solution)/shard_map/ppermute | solution.py:16
  4.9 2.1 %collective-permute-start = (f32[3,1,32,128]{3,2,1,0:T(8,128)S(1)}, f32[3,1,32,128]{3,2,1,0:T(8,128)S(1)}, u32[]{:S(2)}, u32[]{:S(2)}) collective-permute-start(f32[3,1,32,128]{3,2,1,0:T(8,128)S(1)} %get-tuple-element.244), channel_id=1, source_target_pairs={{8,0},{16,8},{24,16},{9,1},{17,9},{25,17},{10,2},{18,10},{26,18},{... | collective-permute-start | bytes 147464 | tf_op jit(solution)/shard_map/ppermute | solution.py:19
  7.0 1.1 slice_reduce_fusion
  8.2 21.5 %while.45 = (s32[]{:T(128)}, f32[8,16,128]{2,1,0:T(8,128)S(1)}, s32[8,16,128]{2,1,0:T(8,128)}, f32[512]{0:T(512)S(1)}, s32[]{:T(128)}) while((s32[]{:T(128)}, f32[8,16,128]{2,1,0:T(8,128)S(1)}, s32[8,16,128]{2,1,0:T(8,128)}, f32[512]{0:T(512)S(1)}, s32[]{:T(128)}) %tuple.106), condition=%wide.region_1.2_spmd.clone, body=%wide.region_0.1_spmd.clone.sunk | while | flops 13631490 | bytes 51269 | solution.py:27
  8.9 2.0 %fusion.54 = f32[1,16,128]{2,0,1:T(1,128)S(1)} fusion(f32[512,1,1]{0,1,2:T(1,128)S(1)} %bitcast.110, s32[16,128]{1,0:T(8,128)S(1)} %dynamic-slice_bitcast_fusion.9), kind=kOutput, calls=%fused_computation.5.clone.1 | convolution fusion | flops 13631488 | bytes 18432 | tf_op jit(solution)/shard_map/while/body/eval_jaxpr/gpc,c->gp/dot_general | solution.py:62
  10.9 0.7 dynamic-slice_bitcast_fusion.9
  11.6 2.0 %fusion.54 = f32[1,16,128]{2,0,1:T(1,128)S(1)} fusion(f32[512,1,1]{0,1,2:T(1,128)S(1)} %bitcast.110, s32[16,128]{1,0:T(8,128)S(1)} %dynamic-slice_bitcast_fusion.9), kind=kOutput, calls=%fused_computation.5.clone.1 | convolution fusion | flops 13631488 | bytes 18432 | tf_op jit(solution)/shard_map/while/body/eval_jaxpr/gpc,c->gp/dot_general | solution.py:62
  13.6 0.7 dynamic-slice_bitcast_fusion.9
  14.3 2.0 %fusion.54 = f32[1,16,128]{2,0,1:T(1,128)S(1)} fusion(f32[512,1,1]{0,1,2:T(1,128)S(1)} %bitcast.110, s32[16,128]{1,0:T(8,128)S(1)} %dynamic-slice_bitcast_fusion.9), kind=kOutput, calls=%fused_computation.5.clone.1 | convolution fusion | flops 13631488 | bytes 18432 | tf_op jit(solution)/shard_map/while/body/eval_jaxpr/gpc,c->gp/dot_general | solution.py:62
  16.2 0.7 dynamic-slice_bitcast_fusion.9
  17.0 2.0 %fusion.54 = f32[1,16,128]{2,0,1:T(1,128)S(1)} fusion(f32[512,1,1]{0,1,2:T(1,128)S(1)} %bitcast.110, s32[16,128]{1,0:T(8,128)S(1)} %dynamic-slice_bitcast_fusion.9), kind=kOutput, calls=%fused_computation.5.clone.1 | convolution fusion | flops 13631488 | bytes 18432 | tf_op jit(solution)/shard_map/while/body/eval_jaxpr/gpc,c->gp/dot_general | solution.py:62
  18.9 0.7 dynamic-slice_bitcast_fusion.9
  19.6 2.0 %fusion.54 = f32[1,16,128]{2,0,1:T(1,128)S(1)} fusion(f32[512,1,1]{0,1,2:T(1,128)S(1)} %bitcast.110, s32[16,128]{1,0:T(8,128)S(1)} %dynamic-slice_bitcast_fusion.9), kind=kOutput, calls=%fused_computation.5.clone.1 | convolution fusion | flops 13631488 | bytes 18432 | tf_op jit(solution)/shard_map/while/body/eval_jaxpr/gpc,c->gp/dot_general | solution.py:62
  21.6 0.7 dynamic-slice_bitcast_fusion.9
  22.3 2.0 %fusion.54 = f32[1,16,128]{2,0,1:T(1,128)S(1)} fusion(f32[512,1,1]{0,1,2:T(1,128)S(1)} %bitcast.110, s32[16,128]{1,0:T(8,128)S(1)} %dynamic-slice_bitcast_fusion.9), kind=kOutput, calls=%fused_computation.5.clone.1 | convolution fusion | flops 13631488 | bytes 18432 | tf_op jit(solution)/shard_map/while/body/eval_jaxpr/gpc,c->gp/dot_general | solution.py:62
  24.3 0.7 dynamic-slice_bitcast_fusion.9
  25.0 2.0 %fusion.54 = f32[1,16,128]{2,0,1:T(1,128)S(1)} fusion(f32[512,1,1]{0,1,2:T(1,128)S(1)} %bitcast.110, s32[16,128]{1,0:T(8,128)S(1)} %dynamic-slice_bitcast_fusion.9), kind=kOutput, calls=%fused_computation.5.clone.1 | convolution fusion | flops 13631488 | bytes 18432 | tf_op jit(solution)/shard_map/while/body/eval_jaxpr/gpc,c->gp/dot_general | solution.py:62
  27.0 0.7 dynamic-slice_bitcast_fusion.9
  27.7 2.0 %fusion.54 = f32[1,16,128]{2,0,1:T(1,128)S(1)} fusion(f32[512,1,1]{0,1,2:T(1,128)S(1)} %bitcast.110, s32[16,128]{1,0:T(8,128)S(1)} %dynamic-slice_bitcast_fusion.9), kind=kOutput, calls=%fused_computation.5.clone.1 | convolution fusion | flops 13631488 | bytes 18432 | tf_op jit(solution)/shard_map/while/body/eval_jaxpr/gpc,c->gp/dot_general | solution.py:62
  31.1 13.5 %while.46 = (s32[]{:T(128)}, f32[8,8,4,256]{3,1,2,0:T(8,128)S(1)}, f32[8,16,8]{1,2,0:T(8,128)S(1)}, f32[8,16,4,128]{3,2,1,0:T(4,128)S(1)}, s32[8,16,128]{2,1,0:T(8,128)}, /*index=5*/s32[]{:T(128)}) while((s32[]{:T(128)}, f32[8,8,4,256]{3,1,2,0:T(8,128)S(1)}, f32[8,16,8]{1,2,0:T(8,128)S(1)}, f32[8,16,4,128]{3,2,1,0:T(4,128)S(1)}, ...), condition=%wide.region_3.4_spmd.clone, body=%wide.region_2.3_spmd.clone.sunk | while | flops 27262976 | bytes 226381 | solution.py:27
  31.9 0.8 fusion.58
  33.5 0.8 fusion.58
  35.2 0.8 fusion.58
  36.9 0.8 fusion.58
  38.6 0.8 fusion.58
  40.3 0.8 fusion.58
  42.0 0.8 fusion.58
  43.7 0.8 fusion.58
  44.7 21.7 %all-reduce.1 = f32[8,4,256]{2,1,0:T(4,128)S(1)} all-reduce(f32[8,4,256]{2,1,0:T(4,128)S(1)} %copy.33), channel_id=3, replica_groups=mesh['body'=4,'mort'=8] {'mort'}, use_global_device_ids=true, to_apply=%region_5.6.clone | all-reduce | flops 8192 | bytes 65536
  68.2 11.0 %all-gather.1 = f32[8,4,256]{2,1,0:T(4,128)S(1)} all-gather(f32[1,4,256]{2,1,0:T(4,128)S(1)} %get-tuple-element.235), channel_id=2, replica_groups=mesh['body'=4,'mort'=8] {'mort'}, dimensions={0}, use_global_device_ids=true | all-gather | bytes 36864 | tf_op jit(solution)/shard_map/all_gather | solution.py:80
  79.7 14.8 %while.47 = (s32[]{:T(128)}, f32[8,16,128]{2,1,0:T(8,128)S(1)}, f32[8,16,4,128]{3,2,1,0:T(4,128)S(1)}, f32[8,16,4,256]{3,1,0,2:T(8,128)S(1)}, s32[8,16,128]{2,1,0:T(8,128)}, /*index=5*/s32[]{:T(128)}) while((s32[]{:T(128)}, f32[8,16,128]{2,1,0:T(8,128)S(1)}, f32[8,16,4,128]{3,2,1,0:T(4,128)S(1)}, f32[8,16,4,256]{3,1,0,2:T(8,128)S(1)}, ...), condition=%wide.region_8.9_spmd.clone, body=%wide.region_7.8_spmd.clone.sunk | while | flops 25704448 | bytes 278613 | solution.py:27
  79.7 0.7 dynamic-slice_bitcast_fusion.11
  80.5 1.1 fusion.60
  82.3 1.1 fusion.60
  84.2 1.1 fusion.60
  86.0 1.1 fusion.60
  87.9 1.1 fusion.60
  89.7 1.1 fusion.60
  91.6 1.1 fusion.60
  93.4 1.1 fusion.60
  94.6 17.8 %while.48 = (s32[]{:T(128)}, f32[8,512]{1,0:T(8,128)S(1)}, s32[8,16,128]{2,1,0:T(8,128)}, f32[8,16,128]{2,1,0:T(8,128)S(1)}, s32[]{:T(128)}, /*index=5*/s32[]{:T(128)}) while((s32[]{:T(128)}, f32[8,512]{1,0:T(8,128)S(1)}, s32[8,16,128]{2,1,0:T(8,128)}, f32[8,16,128]{2,1,0:T(8,128)S(1)}, s32[]{:T(128)}, ...), condition=%wide.region_10.11_spmd.clone, body=%wide.region_9.10_spmd.clone.sunk | while | flops 13631490 | bytes 55377 | solution.py:27
  94.6 0.8 dynamic-slice_bitcast_fusion.12
  95.4 1.4 fusion.62
  97.6 1.4 fusion.62
  99.8 1.4 fusion.62
  102.0 1.4 fusion.62
  104.3 1.4 fusion.62
  106.5 1.4 fusion.62
  108.7 1.4 fusion.62
  110.9 1.4 fusion.62
  112.5 1.1 pad_maximum_fusion.3
  113.6 2.1 %collective-permute-start.2 = (f32[3,18,1,128]{3,2,1,0:T(1,128)S(1)}, f32[3,18,1,128]{3,2,1,0:T(1,128)S(1)}, u32[]{:S(2)}, u32[]{:S(2)}) collective-permute-start(f32[3,18,1,128]{3,2,1,0:T(1,128)S(1)} %get-tuple-element.240), channel_id=1, source_target_pairs={{1,0},{2,1},{3,2},{4,3},{5,4},{6,5},{7,6},{9,8},{10,9},{11,10},{12... | collective-permute-start | bytes 82952 | tf_op jit(solution)/shard_map/ppermute | solution.py:19
  115.7 4.4 %collective-permute-start.3 = (f32[3,18,1,128]{3,2,1,0:T(1,128)S(1)}, f32[3,18,1,128]{3,2,1,0:T(1,128)S(1)}, u32[]{:S(2)}, u32[]{:S(2)}) collective-permute-start(f32[3,18,1,128]{3,2,1,0:T(1,128)S(1)} %get-tuple-element.239), channel_id=1, source_target_pairs={{0,1},{1,2},{2,3},{3,4},{4,5},{5,6},{6,7},{8,9},{9,10},{10,11},{11... | collective-permute-start | bytes 82952 | tf_op jit(solution)/shard_map/ppermute | solution.py:16
  120.1 2.2 %copy.26 = f32[3,16,32,128]{2,1,3,0:T(8,128)} copy(f32[3,16,32,128]{3,2,1,0:T(8,128)S(1)} %copy-done) | data formatting | bytes 1572864 | tf_op args[0]
  122.4 3.2 %copy.32 = f32[3,16,32,128]{2,1,3,0:T(8,128)} copy(f32[3,16,32,128]{3,2,1,0:T(8,128)} %param.22) | data formatting | bytes 1572864 | tf_op args[1]
  125.6 1.3 copy.25
  127.0 2.2 %copy.46 = f32[3,16,32,128]{2,1,3,0:T(8,128)} copy(f32[3,16,32,128]{3,2,1,0:T(8,128)S(1)} %copy-done.1) | data formatting | bytes 1572864
  129.3 2.2 %copy.47 = f32[3,16,32,128]{2,1,3,0:T(8,128)} copy(f32[3,16,32,128]{3,2,1,0:T(8,128)S(1)} %get-tuple-element.241) | data formatting | bytes 1572864
  131.7 2.3 %copy.48 = f32[3,16,32,128]{2,1,3,0:T(8,128)} copy(f32[3,16,32,128]{3,2,1,0:T(8,128)S(1)} %get-tuple-element.237) | data formatting | bytes 1572864
  134.0 2.3 %copy.49 = f32[3,16,32,128]{2,1,3,0:T(8,128)} copy(f32[3,16,32,128]{3,2,1,0:T(8,128)S(1)} %get-tuple-element.238) | data formatting | bytes 1572864
  136.4 3.4 %copy.31 = f32[3,18,34,128]{2,1,3,0:T(8,128)} copy(f32[3,18,34,128]{3,2,1,0:T(8,128)S(1)} %pad_maximum_fusion) | data formatting | bytes 1880064 | tf_op jit(solution)/shard_map/concatenate | solution.py:20
  139.8 10.4 %fusion.31 = f32[3,16,32,128]{2,1,3,0:T(8,128)S(1)} fusion(f32[3,16,32,128]{2,1,3,0:T(8,128)} %copy.32, f32[3,18,34,128]{2,1,3,0:T(8,128)} %copy.31, f32[3,16,32,128]{2,1,3,0:T(8,128)} %copy.49, f32[3,16,32,128]{2,1,3,0:T(8,128)} %copy.48, f32[3,16,32,128]{2,1,3,0:T(8,128)} %copy.46, f32[3,16,32,128]{2,1,3,0:T(8,128)} %copy.47, f32[3,16,32,128]{2,1,3,0:T(8,128)} %copy.26, ...), kind=kLoop, calls=%fused_computation.43 | loop fusion | flops 1572864 | bytes 6707200 | tf_op jit(solution)/shard_map/sub | solution.py:102
  150.3 1.9 %copy.36 = f32[3,16,32,128]{3,2,1,0:T(8,128)} copy(f32[3,16,32,128]{2,1,3,0:T(8,128)S(1)} %fusion.35) | data formatting | bytes 1572864
  (123 shorter events, 22.5 us)
Async XLA Ops:
  0.6 29.6 %copy-start.8 = (s32[128,1]{0,1:T(1,128)S(1)}, s32[128,1]{0,1:T(1,128)}, u32[]{:S(2)}) copy-start(s32[128,1]{0,1:T(1,128)} %param.29) | copy-start | bytes 1540
  0.6 30.4 %copy-start.5 = (f32[128,128]{1,0:T(8,128)S(1)}, f32[128,128]{1,0:T(8,128)}, u32[]{:S(2)}) copy-start(f32[128,128]{1,0:T(8,128)} %param.24) | copy-start | bytes 196612
  1.5 29.5 %copy-start.2 = (f32[128,128]{1,0:T(8,128)S(1)}, f32[128,128]{1,0:T(8,128)}, u32[]{:S(2)}) copy-start(f32[128,128]{1,0:T(8,128)} %param.25) | copy-start | bytes 196612
  1.5 29.5 %copy-start.3 = (f32[128,4,128]{2,1,0:T(4,128)S(1)}, f32[128,4,128]{2,1,0:T(4,128)}, u32[]{:S(2)}) copy-start(f32[128,4,128]{2,1,0:T(4,128)} %param.26) | copy-start | bytes 786436
  1.5 110.9 %collective-permute-start.1 = (f32[3,1,32,128]{3,2,1,0:T(8,128)S(1)}, f32[3,1,32,128]{3,2,1,0:T(8,128)S(1)}, u32[]{:S(2)}, u32[]{:S(2)}) collective-permute-start(f32[3,1,32,128]{3,2,1,0:T(8,128)S(1)} %get-tuple-element.245), channel_id=1, source_target_pairs={{0,8},{8,16},{16,24},{1,9},{9,17},{17,25},{2,10},{10,18},{18,26},{... | collective-permute-start | bytes 147464 | tf_op jit(solution)/shard_map/ppermute | solution.py:16
  4.9 107.6 %collective-permute-start = (f32[3,1,32,128]{3,2,1,0:T(8,128)S(1)}, f32[3,1,32,128]{3,2,1,0:T(8,128)S(1)}, u32[]{:S(2)}, u32[]{:S(2)}) collective-permute-start(f32[3,1,32,128]{3,2,1,0:T(8,128)S(1)} %get-tuple-element.244), channel_id=1, source_target_pairs={{8,0},{16,8},{24,16},{9,1},{17,9},{25,17},{10,2},{18,10},{26,18},{... | collective-permute-start | bytes 147464 | tf_op jit(solution)/shard_map/ppermute | solution.py:19
  29.7 36.7 %copy-start.9 = (u32[32]{0:T(128)S(1)}, u32[32]{0:T(128)}, u32[]{:S(2)}) copy-start(u32[32]{0:T(128)} %constant.89) | copy-start | bytes 388
  29.7 37.9 %copy-start.6 = (f32[4,4,256]{2,1,0:T(4,128)S(1)}, f32[4,4,256]{2,1,0:T(4,128)}, u32[]{:S(2)}) copy-start(f32[4,4,256]{2,1,0:T(4,128)} %param.31) | copy-start | bytes 49156
  29.7 37.9 %copy-start.7 = (f32[4,256]{1,0:T(4,128)S(1)}, f32[4,256]{1,0:T(4,128)}, u32[]{:S(2)}) copy-start(f32[4,256]{1,0:T(4,128)} %param.30) | copy-start | bytes 12292
  94.6 17.9 %copy-start = (f32[3,16,32,128]{3,2,1,0:T(8,128)S(1)}, f32[3,16,32,128]{3,2,1,0:T(8,128)}, u32[]{:S(2)}) copy-start(f32[3,16,32,128]{3,2,1,0:T(8,128)} %param.21) | copy-start | bytes 2359300
  112.4 7.7 %copy-start.4 = (f32[16,32,128]{2,1,0:T(8,128)S(1)}, f32[16,32,128]{2,1,0:T(8,128)}, u32[]{:S(2)}) copy-start(f32[16,32,128]{2,1,0:T(8,128)} %param.23) | copy-start | bytes 786436
  113.6 17.9 %collective-permute-start.2 = (f32[3,18,1,128]{3,2,1,0:T(1,128)S(1)}, f32[3,18,1,128]{3,2,1,0:T(1,128)S(1)}, u32[]{:S(2)}, u32[]{:S(2)}) collective-permute-start(f32[3,18,1,128]{3,2,1,0:T(1,128)S(1)} %get-tuple-element.240), channel_id=1, source_target_pairs={{1,0},{2,1},{3,2},{4,3},{5,4},{6,5},{7,6},{9,8},{10,9},{11,10},{12... | collective-permute-start | bytes 82952 | tf_op jit(solution)/shard_map/ppermute | solution.py:19
  115.7 15.8 %collective-permute-start.3 = (f32[3,18,1,128]{3,2,1,0:T(1,128)S(1)}, f32[3,18,1,128]{3,2,1,0:T(1,128)S(1)}, u32[]{:S(2)}, u32[]{:S(2)}) collective-permute-start(f32[3,18,1,128]{3,2,1,0:T(1,128)S(1)} %get-tuple-element.239), channel_id=1, source_target_pairs={{0,1},{1,2},{2,3},{3,4},{4,5},{5,6},{6,7},{8,9},{9,10},{10,11},{11... | collective-permute-start | bytes 82952 | tf_op jit(solution)/shard_map/ppermute | solution.py:16
  122.4 4.7 %copy-start.1 = (f32[3,16,32,128]{3,2,1,0:T(8,128)S(1)}, f32[3,16,32,128]{3,2,1,0:T(8,128)}, u32[]{:S(2)}) copy-start(f32[3,16,32,128]{3,2,1,0:T(8,128)} %get-tuple-element.242) | copy-start | bytes 2359300
where the time goes:
time: 154 us; the launch traced here: 152 us
  local copies, waits for them, and re-layouts  48.4 us (31%)
  matrix products  44.1 us (29%)
  blocking collectives  32.7 us (21%)
  other arithmetic  13.4 us (9%)
  starting transfers between devices  11.9 us (8%)
    unnamed x1, blocking collectives  21.7 us
    unnamed x30, local copies, waits for them, and re-layouts  17.5 us
    dot_general x8, matrix products, lookup(): return jnp.einsum('gpc,c->gp', onehot, surface, precision=exact)  15.8 us
    dot_general x8, matrix products, spread(): return jnp.einsum('gpc,gp->c', onehot, loads, precision=exact)  11.5 us
    all_gather x1, blocking collectives, body(): changes = lax.all_gather(change[None], 'mort', axis=0, tiled=True)  11 us
    sub x1, other arithmetic, body(): residual = body_load - stiff_force  10.4 us
    dot_general x8, matrix products, picked(): return jnp.einsum('gps,gks,gkp->gp', onehot, table, basis, precision=exact)  8.74 us
    ppermute x2, starting transfers between devices, extended(): lax.ppermute(lax.slice_in_dim(block, block.shape[dim] - width, None, axis...  7.73 us
  transfers between devices with their start and end apart: 4, of which 0 were waited for; matrix products, arithmetic and copies ran while one was open for 55% of the time, Pallas kernels for 0%

commit v1 on v0

v1 whole, which is shorter than its diff:
```python
import functools

import jax
import jax.numpy as jnp
from jax import lax
from jax.experimental import pallas as pl
from jax.experimental.pallas import tpu as pltpu
from jax.sharding import PartitionSpec as P

LANES = 128
ROWS = 8
PIECES = 3
VMEM = pl.BlockSpec(memory_space=pltpu.VMEM)
SMEM = pl.BlockSpec(memory_space=pltpu.SMEM)
ANY = pl.BlockSpec(memory_space=pl.ANY)


def pieces_of(value):
    out = []
    for _ in range(PIECES - 1):
        part = value.astype(jnp.bfloat16).astype(jnp.float32)
        out.append(part)
        value = value - part
    return out + [value]


def lane_gather(table, index):
    return jnp.take_along_axis(table, index, axis=1, mode="promise_in_bounds")


def gather_rows(rows, index):
    row, lane = index // LANES, index % LANES
    value = None
    for number, piece in enumerate(rows):
        got = lane_gather(jnp.broadcast_to(piece, index.shape), lane)
        value = got if value is None else jnp.where(row == number, got, value)
    return value


def nt_dot(a, b):
    return lax.dot_general(a, b, (((1,), (1,)), ((), ())), preferred_element_type=jnp.float32)


def shares_kernel(
    count, modes, disp_ref, gap_ref, weight_ref, basis_ref, cell_ref, seg_ref, owner_ref,
    partial_ref, face_ref, terms, acc,
):
    _, cells_x, cells_y, _ = disp_ref.shape
    blocks = gap_ref.shape[0]
    segments = partial_ref.shape[2]
    pad = terms.shape[0] // blocks
    face_ref[0] = disp_ref[:, :, cells_y - 1, :]
    face_ref[1] = disp_ref[:, :, 0, :]
    per = LANES // cells_y
    lane = lax.broadcasted_iota(jnp.int32, (cells_y, LANES), 1)
    columns = []
    for j in range(per):
        column = jnp.zeros((cells_y, LANES), jnp.float32)
        for r in range(cells_x // per):
            values = disp_ref[2, r * per + j, :, :][:, 0:1]
            column = jnp.where(lane == r, values, column)
        columns.append(column)
    table = jnp.concatenate(columns, axis=0).T
    surface = [table[r : r + 1, :] for r in range(cells_x // per)]

    zero = jnp.zeros((ROWS, LANES), jnp.float32)

    def prepare(t, _):
        first = pl.multiple_of(t * ROWS, ROWS)
        rows = pl.ds(first, ROWS)
        gap = gap_ref[rows, :] + gather_rows(surface, cell_ref[rows, :])
        weights = weight_ref[rows, :]
        for k in range(modes):
            basis = basis_ref[pl.ds(first * modes + k, ROWS, stride=modes), :]
            for s, piece in enumerate(pieces_of(weights * basis * gap)):
                terms[pl.ds(first * pad + s * modes + k, ROWS, stride=pad), :] = piece
        for k in range(PIECES * modes, pad):
            terms[pl.ds(first * pad + k, ROWS, stride=pad), :] = zero
        return 0

    lax.fori_loop(0, blocks // ROWS, prepare, 0, unroll=2)
    acc[...] = jnp.zeros_like(acc)
    ids = lax.broadcasted_iota(jnp.int32, (segments, LANES), 0)

    def add(t, _):
        first = pl.multiple_of(t * ROWS, ROWS)
        left, right = [], []
        for i in range(ROWS):
            item = terms[pl.ds(pl.multiple_of((first + i) * pad, pad), pad), :].astype(jnp.bfloat16)
            owner = owner_ref[first + i]
            left.append(
                jnp.concatenate(
                    [jnp.where(owner == o, item, jnp.zeros_like(item)) for o in range(count)], axis=0
                )
            )
            segs = seg_ref[pl.ds(first + i, 1), :]
            right.append(jnp.where(segs == ids, 1.0, 0.0).astype(jnp.bfloat16))
        acc[...] += nt_dot(jnp.concatenate(left, axis=1), jnp.concatenate(right, axis=1))
        return 0

    lax.fori_loop(0, blocks // ROWS, add, 0)
    for o in range(count):
        total = acc[pl.ds(o * pad, pad), :]
        value = total[0:modes]
        for s in range(1, PIECES):
            value = value + total[s * modes : (s + 1) * modes]
        partial_ref[o] = value


def exchange_kernel(
    partial_ref, mult_ref, inv_ref, face_ref, disp_ref,
    changes_ref, updated_ref, xhalo_ref, yhalo_ref,
    landed, send1, recv1, send2, recv2, sendx, recvx, sendy, recvy,
):
    count, nb = lax.axis_size("mort"), lax.axis_size("body")
    me, mb = lax.axis_index("mort"), lax.axis_index("body")
    cells_x = disp_ref.shape[1]
    barrier = pltpu.get_barrier_semaphore()
    for j in range(1, count):
        pl.semaphore_signal(
            barrier, inc=1, device_id={"mort": lax.rem(me + j, count)},
            device_id_type=pl.DeviceIdType.MESH,
        )
    for j in (1, nb - 1):
        pl.semaphore_signal(
            barrier, inc=1, device_id={"body": lax.rem(mb + j, nb)},
            device_id_type=pl.DeviceIdType.MESH,
        )
    pl.semaphore_wait(barrier, count + 1)

    def share(j):
        target = lax.rem(me + j, count)
        return pltpu.make_async_remote_copy(
            src_ref=partial_ref.at[target], dst_ref=landed.at[j],
            send_sem=send1.at[j], recv_sem=recv1.at[j],
            device_id={"mort": target}, device_id_type=pl.DeviceIdType.MESH,
        )

    def xcopy(side):
        return pltpu.make_async_remote_copy(
            src_ref=disp_ref.at[:, cells_x - 1 if side == 0 else 0],
            dst_ref=xhalo_ref.at[side],
            send_sem=sendx.at[side], recv_sem=recvx.at[side],
            device_id={"body": lax.rem(mb + (1 if side == 0 else nb - 1), nb)},
            device_id_type=pl.DeviceIdType.MESH,
        )

    def ycopy(side):
        return pltpu.make_async_remote_copy(
            src_ref=face_ref.at[side], dst_ref=yhalo_ref.at[side],
            send_sem=sendy.at[side], recv_sem=recvy.at[side],
            device_id={"mort": lax.rem(me + (1 if side == 0 else count - 1), count)},
            device_id_type=pl.DeviceIdType.MESH,
        )

    shares = [share(j) for j in range(1, count)]
    for copy in shares:
        copy.start()
    halos = []
    for make, place, size, ref in ((xcopy, mb, nb, xhalo_ref), (ycopy, me, count, yhalo_ref)):
        for side in range(2):
            sends = place < size - 1 if side == 0 else place > 0
            takes = place > 0 if side == 0 else place < size - 1
            halos.append((make, side, sends, takes))

            @pl.when(sends)
            def _():
                make(side).start()

            @pl.when(jnp.logical_not(takes))
            def _():
                ref[side] = jnp.zeros(ref.shape[1:], ref.dtype)

    total = partial_ref[me]
    for j in range(1, count):
        shares[j - 1].wait_recv()
        total = total + landed[j]
    applied = inv_ref[:, 0, :] * total[0:1, :]
    for l in range(1, total.shape[0]):
        applied = applied + inv_ref[:, l, :] * total[l : l + 1, :]
    old = mult_ref[...]
    updated = jnp.maximum(old - applied, 0.0)
    updated_ref[...] = updated
    changes_ref[me] = updated - old

    def spread(j):
        return pltpu.make_async_remote_copy(
            src_ref=changes_ref.at[me], dst_ref=changes_ref.at[me],
            send_sem=send2.at[j], recv_sem=recv2.at[j],
            device_id={"mort": lax.rem(me + j, count)}, device_id_type=pl.DeviceIdType.MESH,
        )

    def arrival(j):
        source = lax.rem(me + count - j, count)
        return pltpu.make_async_remote_copy(
            src_ref=changes_ref.at[me], dst_ref=changes_ref.at[source],
            send_sem=send2.at[j], recv_sem=recv2.at[j],
            device_id={"mort": lax.rem(me + j, count)}, device_id_type=pl.DeviceIdType.MESH,
        )

    for j in range(1, count):
        spread(j).start()
    for copy in shares:
        copy.wait_send()
    for make, side, sends, takes in halos:

        @pl.when(sends)
        def _():
            make(side).wait_send()

        @pl.when(takes)
        def _():
            make(side).wait_recv()

    for j in range(1, count):
        spread(j).wait_send()
        arrival(j).wait_recv()


def residual_kernel(
    disp_ref, load_ref, stiff_ref, weight_ref, basis_ref, cell_ref, seg_ref, owner_ref,
    changes_ref, new_ref, xhalo_ref, yhalo_ref,
    out_ref, updated_ref, loads,
):
    parts, cells_x, cells_y, nz = disp_ref.shape
    blocks = weight_ref.shape[0]
    count, modes, segments = changes_ref.shape
    updated_ref[...] = new_ref[...]

    def pressures(t, _):
        first = pl.multiple_of(t * ROWS, ROWS)
        rows = pl.ds(first, ROWS)
        owner = jnp.broadcast_to(owner_ref[rows, :], (ROWS, LANES))
        segs = seg_ref[rows, :]
        masks = [owner == o for o in range(count)]
        pressure = None
        for k in range(modes):
            pieces = []
            for h in range(segments // LANES):
                piece = jnp.zeros((ROWS, LANES), jnp.float32)
                for o in range(count):
                    row = changes_ref[o, k : k + 1, h * LANES : (h + 1) * LANES]
                    piece = jnp.where(masks[o], row, piece)
                pieces.append(piece)
            basis = basis_ref[pl.ds(first * modes + k, ROWS, stride=modes), :]
            term = basis * gather_rows(pieces, segs)
            pressure = term if pressure is None else pressure + term
        loads[rows, :] = weight_ref[rows, :] * pressure
        return 0

    lax.fori_loop(0, blocks // ROWS, pressures, 0)
    xs = lax.broadcasted_iota(jnp.int32, (cells_x, LANES), 0)
    ys = lax.broadcasted_iota(jnp.int32, (cells_y, LANES), 0)

    def spread(t, acc):
        first = t * ROWS
        left, right = [], []
        for i in range(ROWS):
            cell = cell_ref[pl.ds(first + i, 1), :]
            at_x, at_y = cell // cells_y, cell % cells_y
            left.append(jnp.where(at_y == ys, 1.0, 0.0).astype(jnp.bfloat16))
            value = jnp.where(at_x == xs, loads[pl.ds(first + i, 1), :], 0.0)
            right.append(jnp.concatenate([p.astype(jnp.bfloat16) for p in pieces_of(value)], axis=0))
        return acc + nt_dot(jnp.concatenate(left, axis=1), jnp.concatenate(right, axis=1))

    acc = lax.fori_loop(
        0, blocks // ROWS, spread, jnp.zeros((cells_y, PIECES * cells_x), jnp.float32)
    )
    lane = lax.broadcasted_iota(jnp.int32, (cells_y, nz), 1)
    row = lax.broadcasted_iota(jnp.int32, (cells_y, nz), 0)
    for x in range(cells_x):
        diagonal = 6.0 + stiff_ref[x]
        for i in range(parts):
            here = disp_ref[i, x]
            low = disp_ref[i, x - 1] if x > 0 else xhalo_ref[0, i]
            high = disp_ref[i, x + 1] if x < cells_x - 1 else xhalo_ref[1, i]
            below = jnp.where(row == 0, yhalo_ref[0, i, x : x + 1, :], pltpu.roll(here, 1, 0))
            above = jnp.where(
                row == cells_y - 1, yhalo_ref[1, i, x : x + 1, :], pltpu.roll(here, cells_y - 1, 0)
            )
            left = jnp.where(lane == 0, 0.0, pltpu.roll(here, 1, 1))
            right = jnp.where(lane == nz - 1, 0.0, pltpu.roll(here, nz - 1, 1))
            beside = high + low + above + below + right + left
            residual = load_ref[i, x] - (diagonal * here - beside)
            if i == 2:
                traction = acc[:, x : x + 1]
                for s in range(1, PIECES):
                    traction = traction + acc[:, s * cells_x + x : s * cells_x + x + 1]
                residual = jnp.where(lane == 0, residual + traction, residual)
            out_ref[i, x] = residual


def body(
    displacement, body_load, stiffness, initial_gap, weights, basis_values, point_cell,
    point_segment, block_owner, multipliers, block_inverse,
):
    parts, cells_x, cells_y, nz = displacement.shape
    blocks, points = initial_gap.shape
    modes, segments = multipliers.shape
    count = lax.axis_size("mort")
    f32 = jnp.float32
    basis = basis_values.reshape(blocks * modes, points)
    pad = -(-PIECES * modes // 16) * 16
    shape = jax.ShapeDtypeStruct
    partial, faces = pl.pallas_call(
        functools.partial(shares_kernel, count, modes),
        name="shares",
        out_shape=(
            shape((count, modes, segments), f32),
            shape((2, parts, cells_x, nz), f32),
        ),
        in_specs=[VMEM] * 6 + [SMEM],
        out_specs=(VMEM, VMEM),
        scratch_shapes=[
            pltpu.VMEM((blocks * pad, LANES), f32),
            pltpu.VMEM((count * pad, segments), f32),
        ],
    )(
        displacement, initial_gap, weights, basis, point_cell, point_segment,
        block_owner.reshape(blocks),
    )
    dma = pltpu.SemaphoreType.DMA
    changes, new, xhalo, yhalo = pl.pallas_call(
        exchange_kernel,
        name="exchange",
        out_shape=(
            shape((count, modes, segments), f32),
            shape((modes, segments), f32),
            shape((2, parts, cells_y, nz), f32),
            shape((2, parts, cells_x, nz), f32),
        ),
        in_specs=[VMEM] * 4 + [ANY],
        out_specs=(VMEM,) * 4,
        scratch_shapes=[pltpu.VMEM((count, modes, segments), f32)]
        + [dma((count,))] * 4
        + [dma((2,))] * 4,
        compiler_params=pltpu.CompilerParams(collective_id=0, has_side_effects=True),
    )(partial, multipliers, block_inverse, faces, displacement)
    return pl.pallas_call(
        residual_kernel,
        name="residual",
        out_shape=(
            shape(displacement.shape, f32),
            shape((modes, segments), f32),
        ),
        in_specs=[VMEM] * 12,
        out_specs=(VMEM, VMEM),
        scratch_shapes=[pltpu.VMEM((blocks, LANES), f32)],
    )(
        displacement, body_load, stiffness, weights, basis, point_cell, point_segment,
        block_owner, changes, new, xhalo, yhalo,
    )


def solution(mesh):
    return jax.shard_map(
        body,
        mesh=mesh,
        in_specs=(
            P(None, "body", "mort", None),
            P(None, "body", "mort", None),
            P("body", "mort", None),
            P(("body", "mort"), None),
            P(("body", "mort"), None),
            P(("body", "mort"), None, None),
            P(("body", "mort"), None),
            P(("body", "mort"), None),
            P(("body", "mort"), None),
            P(None, ("body", "mort")),
            P(None, None, ("body", "mort")),
        ),
        out_specs=(P(None, "body", "mort", None), P(None, ("body", "mort"))),
        check_vma=False,
    )
```

time: 154 us -> 32.1 us (0.21)
  the two profiles are of different devices: /device:TPU:19 before, /device:TPU:0 now
where the time goes in v1:
time: 32.1 us; the launch traced here: 31.9 us
  Pallas kernels  29.8 us (93%)
  local copies, waits for them, and re-layouts  1.39 us (4%)
  between operations  0.65 us (2%)
    pallas_call x1, Pallas kernels, body(): pl.pallas_call(exchange_kernel, name='exchange', out_shape=(shape((count,...  13.3 us
    pallas_call x1, Pallas kernels, body(): pl.pallas_call(residual_kernel, name='residual', out_shape=(shape(displac...  8.47 us
    pallas_call x1, Pallas kernels, body(): pl.pallas_call(functools.partial(shares_kernel, count, modes), name='shar...  8.03 us
    unnamed x3, local copies, waits for them, and re-layouts  1.39 us

profile of v1, /device:TPU:0, one launch (start us, length us, event | category | flops | bytes accessed | tf_op | source)
XLA Modules:
  0.0 31.9 jit_solution(2687622861624934074)
XLA Ops:
  0.6 0.0 copy-start
  0.6 0.6 %copy-done = s32[128,1]{0,1:T(1,128)S(1)} copy-done((s32[128,1]{0,1:T(1,128)S(1)}, s32[128,1]{0,1:T(1,128)}, u32[]{:S(2)}) %copy-start) | copy-done | bytes 536
  1.3 0.7 %copy.13.owner_ref = s32[128,1]{1,0:T(8,128)} copy(s32[128,1]{0,1:T(1,128)S(1)} %copy-done) | data formatting | bytes 1024 | tf_op args[8]
  2.0 8.0 %shares.1 = (f32[8,4,256]{2,1,0:T(4,128)}, f32[2,3,16,128]{3,2,1,0:T(8,128)}) custom-call(f32[3,16,32,128]{3,2,1,0:T(8,128)} %disp_ref.5, f32[128,128]{1,0:T(8,128)} %gap_ref.1, f32[128,128]{1,0:T(8,128)} %weight_ref.3, f32[512,128]{1,0:T(8,128)} %bitcast.2, s32[128,128]{1,0:T(8,128)} %cell_ref.3, s32[128,128]{1,0:T(8,128)} %seg_ref.3, s32[128]{0:T(128)} %bitcast.4), custom_call_target="tpu_custom_call" | custom-call | tf_op jit(solution)/shard_map/shares/pallas_call | solution.py:305
  10.1 13.3 %exchange.1 = (f32[8,4,256]{2,1,0:T(4,128)}, f32[4,256]{1,0:T(4,128)}, f32[2,3,32,128]{3,2,1,0:T(8,128)}, f32[2,3,16,128]{3,2,1,0:T(8,128)}) custom-call(f32[8,4,256]{2,1,0:T(4,128)} %get-tuple-element.8.partial_ref, f32[4,256]{1,0:T(4,128)} %mult_ref.1, f32[4,4,256]{2,1,0:T(4,128)} %inv_ref.1, f32[2,3,16,128]{3,2,1,0:T(8,128)} %get-tuple-element.9.face_ref, ...), custom_call_target="tpu_custom_call" | custom-call | tf_op jit(solution)/shard_map/exchange/pallas_call | solution.py:323
  23.4 8.5 %residual.1 = (f32[3,16,32,128]{3,2,1,0:T(8,128)}, f32[4,256]{1,0:T(4,128)}) custom-call(f32[3,16,32,128]{3,2,1,0:T(8,128)} %disp_ref.5, f32[3,16,32,128]{3,2,1,0:T(8,128)} %load_ref.1, f32[16,32,128]{2,1,0:T(8,128)} %stiff_ref.1, f32[128,128]{1,0:T(8,128)} %weight_ref.3, f32[512,128]{1,0:T(8,128)} %bitcast.3, s32[128,128]{1,0:T(8,128)} %cell_ref.3, ...), custom_call_target="tpu_custom_call" | custom-call | tf_op jit(solution)/shard_map/residual/pallas_call | solution.py:339
Async XLA Ops:
  0.6 0.7 %copy-start = (s32[128,1]{0,1:T(1,128)S(1)}, s32[128,1]{0,1:T(1,128)}, u32[]{:S(2)}) copy-start(s32[128,1]{0,1:T(1,128)} %param.19) | copy-start | bytes 1540

commit v2 on v1

--- a/solution.py
+++ b/solution.py
@@ -1,5 +1,3 @@
-import functools
-
 import jax
 import jax.numpy as jnp
 from jax import lax
@@ -12,7 +10,6 @@
 PIECES = 3
 VMEM = pl.BlockSpec(memory_space=pltpu.VMEM)
 SMEM = pl.BlockSpec(memory_space=pltpu.SMEM)
-ANY = pl.BlockSpec(memory_space=pl.ANY)
 
 
 def pieces_of(value):
@@ -41,16 +38,15 @@
     return lax.dot_general(a, b, (((1,), (1,)), ((), ())), preferred_element_type=jnp.float32)
 
 
-def shares_kernel(
-    count, modes, disp_ref, gap_ref, weight_ref, basis_ref, cell_ref, seg_ref, owner_ref,
-    partial_ref, face_ref, terms, acc,
+def make_shares(
+    disp_ref, gap_ref, weight_ref, basis_ref, cell_ref, seg_ref, owner_ref,
+    partial_ref, terms, acc,
 ):
+    count, modes, _ = partial_ref.shape
     _, cells_x, cells_y, _ = disp_ref.shape
     blocks = gap_ref.shape[0]
     segments = partial_ref.shape[2]
     pad = terms.shape[0] // blocks
-    face_ref[0] = disp_ref[:, :, cells_y - 1, :]
-    face_ref[1] = disp_ref[:, :, 0, :]
     per = LANES // cells_y
     lane = lax.broadcasted_iota(jnp.int32, (cells_y, LANES), 1)
     columns = []
@@ -108,9 +104,9 @@
 
 
 def exchange_kernel(
-    partial_ref, mult_ref, inv_ref, face_ref, disp_ref,
+    disp_ref, gap_ref, weight_ref, basis_ref, cell_ref, seg_ref, owner_ref, mult_ref, inv_ref,
     changes_ref, updated_ref, xhalo_ref, yhalo_ref,
-    landed, send1, recv1, send2, recv2, sendx, recvx, sendy, recvy,
+    terms, acc, partial_ref, face_ref, landed, send1, recv1, send2, recv2, sendx, recvx, sendy, recvy,
 ):
     count, nb = lax.axis_size("mort"), lax.axis_size("body")
     me, mb = lax.axis_index("mort"), lax.axis_index("body")
@@ -126,6 +122,13 @@
             barrier, inc=1, device_id={"body": lax.rem(mb + j, nb)},
             device_id_type=pl.DeviceIdType.MESH,
         )
+    cells_y = disp_ref.shape[2]
+    face_ref[0] = disp_ref[:, :, cells_y - 1, :]
+    face_ref[1] = disp_ref[:, :, 0, :]
+    make_shares(
+        disp_ref, gap_ref, weight_ref, basis_ref, cell_ref, seg_ref, owner_ref,
+        partial_ref, terms, acc,
+    )
     pl.semaphore_wait(barrier, count + 1)
 
     def share(j):
@@ -220,17 +223,18 @@
 def residual_kernel(
     disp_ref, load_ref, stiff_ref, weight_ref, basis_ref, cell_ref, seg_ref, owner_ref,
     changes_ref, new_ref, xhalo_ref, yhalo_ref,
-    out_ref, updated_ref, loads,
+    out_ref, updated_ref, loads, owners,
 ):
     parts, cells_x, cells_y, nz = disp_ref.shape
     blocks = weight_ref.shape[0]
     count, modes, segments = changes_ref.shape
     updated_ref[...] = new_ref[...]
+    owners[...] = jnp.broadcast_to(owner_ref[...], (LANES, blocks)).T
 
     def pressures(t, _):
         first = pl.multiple_of(t * ROWS, ROWS)
         rows = pl.ds(first, ROWS)
-        owner = jnp.broadcast_to(owner_ref[rows, :], (ROWS, LANES))
+        owner = owners[rows, :]
         segs = seg_ref[rows, :]
         masks = [owner == o for o in range(count)]
         pressure = None
@@ -302,23 +306,6 @@
     basis = basis_values.reshape(blocks * modes, points)
     pad = -(-PIECES * modes // 16) * 16
     shape = jax.ShapeDtypeStruct
-    partial, faces = pl.pallas_call(
-        functools.partial(shares_kernel, count, modes),
-        name="shares",
-        out_shape=(
-            shape((count, modes, segments), f32),
-            shape((2, parts, cells_x, nz), f32),
-        ),
-        in_specs=[VMEM] * 6 + [SMEM],
-        out_specs=(VMEM, VMEM),
-        scratch_shapes=[
-            pltpu.VMEM((blocks * pad, LANES), f32),
-            pltpu.VMEM((count * pad, segments), f32),
-        ],
-    )(
-        displacement, initial_gap, weights, basis, point_cell, point_segment,
-        block_owner.reshape(blocks),
-    )
     dma = pltpu.SemaphoreType.DMA
     changes, new, xhalo, yhalo = pl.pallas_call(
         exchange_kernel,
@@ -329,26 +316,38 @@
             shape((2, parts, cells_y, nz), f32),
             shape((2, parts, cells_x, nz), f32),
         ),
-        in_specs=[VMEM] * 4 + [ANY],
+        in_specs=[VMEM] * 6 + [SMEM] + [VMEM] * 2,
         out_specs=(VMEM,) * 4,
-        scratch_shapes=[pltpu.VMEM((count, modes, segments), f32)]
+        scratch_shapes=[
+            pltpu.VMEM((blocks * pad, LANES), f32),
+            pltpu.VMEM((count * pad, segments), f32),
+            pltpu.VMEM((count, modes, segments), f32),
+            pltpu.VMEM((2, parts, cells_x, nz), f32),
+            pltpu.VMEM((count, modes, segments), f32),
+        ]
         + [dma((count,))] * 4
         + [dma((2,))] * 4,
-        compiler_params=pltpu.CompilerParams(collective_id=0, has_side_effects=True),
-    )(partial, multipliers, block_inverse, faces, displacement)
+        compiler_params=pltpu.CompilerParams(
+            vmem_limit_bytes=8 << 20, collective_id=0, has_side_effects=True
+        ),
+    )(
+        displacement, initial_gap, weights, basis, point_cell, point_segment,
+        block_owner.reshape(blocks), multipliers, block_inverse,
+    )
     return pl.pallas_call(
         residual_kernel,
         name="residual",
+        compiler_params=pltpu.CompilerParams(vmem_limit_bytes=8 << 20),
         out_shape=(
             shape(displacement.shape, f32),
             shape((modes, segments), f32),
         ),
         in_specs=[VMEM] * 12,
         out_specs=(VMEM, VMEM),
-        scratch_shapes=[pltpu.VMEM((blocks, LANES), f32)],
+        scratch_shapes=[pltpu.VMEM((blocks, LANES), f32), pltpu.VMEM((blocks, LANES), jnp.int32)],
     )(
         displacement, body_load, stiffness, weights, basis, point_cell, point_segment,
-        block_owner, changes, new, xhalo, yhalo,
+        block_owner.reshape(1, blocks), changes, new, xhalo, yhalo,
     )
 
 

time: 32.1 us -> 29.9 us (0.931)
  Pallas kernels: 29.8 us -> 20.9 us
  local copies, waits for them, and re-layouts: 1.39 us -> 7.79 us
    pallas_call x2 -> x1, Pallas kernels: 16.5 us -> 5.94 us  [body(): pl.pallas_call(residual_kernel, name='residual', compiler_params=pltpu.Co...]
    unnamed x3 -> x28, local copies, waits for them, and re-layouts: 1.39 us -> 7.79 us
    pallas_call x1, Pallas kernels: 13.3 us -> 15 us  [body(): pl.pallas_call(exchange_kernel, name='exchange', out_shape=(shape((count,...]
where the time goes in v2:
time: 29.9 us; the launch traced here: 29.4 us
  Pallas kernels  20.9 us (70%)
  local copies, waits for them, and re-layouts  7.79 us (26%)
  between operations  0.71 us (2%)
    pallas_call x1, Pallas kernels, body(): pl.pallas_call(exchange_kernel, name='exchange', out_shape=(shape((count,...  15 us
    unnamed x28, local copies, waits for them, and re-layouts  7.79 us
    pallas_call x1, Pallas kernels, body(): pl.pallas_call(residual_kernel, name='residual', compiler_params=pltpu.Co...  5.94 us

profile of v2, /device:TPU:0, one launch (start us, length us, event | category | flops | bytes accessed | tf_op | source)
XLA Modules:
  0.0 29.4 jit_solution(12066185976128497461)
XLA Ops:
  0.6 0.0 copy-start.12
  0.6 0.0 copy-start.13
  0.7 0.7 %copy-done.12 = f32[4,256]{1,0:T(4,128)S(1)} copy-done((f32[4,256]{1,0:T(4,128)S(1)}, f32[4,256]{1,0:T(4,128)}, u32[]{:S(2)}) %copy-start.12) | copy-done | bytes 4120
  1.3 0.0 copy-done.13
  1.3 0.0 copy-start
  1.3 1.1 %copy-done = f32[3,16,32,128]{3,2,1,0:T(8,128)S(1)} copy-done((f32[3,16,32,128]{3,2,1,0:T(8,128)S(1)}, f32[3,16,32,128]{3,2,1,0:T(8,128)}, u32[]{:S(2)}) %copy-start) | copy-done | bytes 786456
  2.5 0.0 copy-start.1
  2.5 0.9 %copy-done.1 = f32[128,4,128]{2,1,0:T(4,128)S(1)} copy-done((f32[128,4,128]{2,1,0:T(4,128)S(1)}, f32[128,4,128]{2,1,0:T(4,128)}, u32[]{:S(2)}) %copy-start.1) | copy-done | bytes 262168
  3.4 0.0 copy-start.4
  3.4 0.8 %copy-done.4 = f32[128,128]{1,0:T(8,128)S(1)} copy-done((f32[128,128]{1,0:T(8,128)S(1)}, f32[128,128]{1,0:T(8,128)}, u32[]{:S(2)}) %copy-start.4) | copy-done | bytes 65560
  4.2 0.0 copy-start.5
  4.3 0.8 %copy-done.5 = s32[128,128]{1,0:T(8,128)S(1)} copy-done((s32[128,128]{1,0:T(8,128)S(1)}, s32[128,128]{1,0:T(8,128)}, u32[]{:S(2)}) %copy-start.5) | copy-done | bytes 65560
  5.1 0.0 copy-start.7
  5.1 0.8 %copy-done.7 = s32[128,128]{1,0:T(8,128)S(1)} copy-done((s32[128,128]{1,0:T(8,128)S(1)}, s32[128,128]{1,0:T(8,128)}, u32[]{:S(2)}) %copy-start.7) | copy-done | bytes 65560
  5.9 0.0 copy-start.10
  5.9 0.8 %copy-done.10 = f32[128,128]{1,0:T(8,128)S(1)} copy-done((f32[128,128]{1,0:T(8,128)S(1)}, f32[128,128]{1,0:T(8,128)}, u32[]{:S(2)}) %copy-start.10) | copy-done | bytes 65560
  6.8 0.0 copy-start.11
  6.8 0.7 %copy-done.11 = f32[4,4,256]{2,1,0:T(4,128)S(1)} copy-done((f32[4,4,256]{2,1,0:T(4,128)S(1)}, f32[4,4,256]{2,1,0:T(4,128)}, u32[]{:S(2)}) %copy-start.11) | copy-done | bytes 16408
  7.5 0.0 copy-start.2
  7.5 0.0 copy-start.3
  7.5 0.0 copy-start.6
  7.5 0.0 copy-start.8
  7.5 15.0 %exchange.1 = (f32[8,4,256]{2,1,0:T(4,128)S(1)}, f32[4,256]{1,0:T(4,128)S(1)}, f32[2,3,32,128]{3,2,1,0:T(8,128)S(1)}, f32[2,3,16,128]{3,2,1,0:T(8,128)S(1)}) custom-call(f32[3,16,32,128]{3,2,1,0:T(8,128)S(1)} %copy-done, f32[128,128]{1,0:T(8,128)S(1)} %copy-done.10, f32[128,128]{1,0:T(8,128)S(1)} %copy-done.4, f32[512,128]{1,0:T(8,128)S(1)} %bitcast.3, ...), custom_call_target="tpu_custom_call" | custom-call | tf_op jit(solution)/shard_map/exchange/pallas_call | solution.py:310
  22.5 0.0 copy-done.2
  22.5 0.0 copy-done.3
  22.5 0.0 copy-done.6
  22.5 0.0 copy-done.8
  22.5 0.0 copy-start.9
  22.6 0.9 %copy-done.9 = f32[16,32,128]{2,1,0:T(8,128)S(1)} copy-done((f32[16,32,128]{2,1,0:T(8,128)S(1)}, f32[16,32,128]{2,1,0:T(8,128)}, u32[]{:S(2)}) %copy-start.9) | copy-done | bytes 262168
  23.5 5.9 %residual.1 = (f32[3,16,32,128]{3,2,1,0:T(8,128)}, f32[4,256]{1,0:T(4,128)}) custom-call(f32[3,16,32,128]{3,2,1,0:T(8,128)S(1)} %copy-done, f32[3,16,32,128]{3,2,1,0:T(8,128)S(1)} %copy-done.3, f32[16,32,128]{2,1,0:T(8,128)S(1)} %copy-done.9, f32[128,128]{1,0:T(8,128)S(1)} %copy-done.4, f32[512,128]{1,0:T(8,128)S(1)} %bitcast.4, s32[128,128]{1,0:T(8,128)S(1)} %copy-done.6, ...), custom_call_target="tpu_custom_call" | custom-call | tf_op jit(solution)/shard_map/residual/pallas_call | solution.py:337
Async XLA Ops:
  0.6 0.7 %copy-start.12 = (f32[4,256]{1,0:T(4,128)S(1)}, f32[4,256]{1,0:T(4,128)}, u32[]{:S(2)}) copy-start(f32[4,256]{1,0:T(4,128)} %mult_ref.1) | copy-start | bytes 12292
  0.6 0.7 %copy-start.13 = (s32[128,1]{0,1:T(1,128)S(1)}, s32[128,1]{0,1:T(1,128)}, u32[]{:S(2)}) copy-start(s32[128,1]{0,1:T(1,128)} %param.19) | copy-start | bytes 1540
  1.3 1.1 %copy-start = (f32[3,16,32,128]{3,2,1,0:T(8,128)S(1)}, f32[3,16,32,128]{3,2,1,0:T(8,128)}, u32[]{:S(2)}) copy-start(f32[3,16,32,128]{3,2,1,0:T(8,128)} %disp_ref.3) | copy-start | bytes 2359300
  2.5 0.9 %copy-start.1 = (f32[128,4,128]{2,1,0:T(4,128)S(1)}, f32[128,4,128]{2,1,0:T(4,128)}, u32[]{:S(2)}) copy-start(f32[128,4,128]{2,1,0:T(4,128)} %param.16) | copy-start | bytes 786436
  3.4 0.8 %copy-start.4 = (f32[128,128]{1,0:T(8,128)S(1)}, f32[128,128]{1,0:T(8,128)}, u32[]{:S(2)}) copy-start(f32[128,128]{1,0:T(8,128)} %weight_ref.3) | copy-start | bytes 196612
  4.2 0.8 %copy-start.5 = (s32[128,128]{1,0:T(8,128)S(1)}, s32[128,128]{1,0:T(8,128)}, u32[]{:S(2)}) copy-start(s32[128,128]{1,0:T(8,128)} %cell_ref.3) | copy-start | bytes 196612
  5.1 0.8 %copy-start.7 = (s32[128,128]{1,0:T(8,128)S(1)}, s32[128,128]{1,0:T(8,128)}, u32[]{:S(2)}) copy-start(s32[128,128]{1,0:T(8,128)} %seg_ref.3) | copy-start | bytes 196612
  5.9 0.8 %copy-start.10 = (f32[128,128]{1,0:T(8,128)S(1)}, f32[128,128]{1,0:T(8,128)}, u32[]{:S(2)}) copy-start(f32[128,128]{1,0:T(8,128)} %gap_ref.1) | copy-start | bytes 196612
  6.8 0.7 %copy-start.11 = (f32[4,4,256]{2,1,0:T(4,128)S(1)}, f32[4,4,256]{2,1,0:T(4,128)}, u32[]{:S(2)}) copy-start(f32[4,4,256]{2,1,0:T(4,128)} %inv_ref.1) | copy-start | bytes 49156
  7.5 15.0 %copy-start.2 = (f32[128,4,128]{2,1,0:T(4,128)S(1)}, f32[128,4,128]{2,1,0:T(4,128)}, u32[]{:S(2)}) copy-start(f32[128,4,128]{2,1,0:T(4,128)} %param.16) | copy-start | bytes 786436
  7.5 15.0 %copy-start.3 = (f32[3,16,32,128]{3,2,1,0:T(8,128)S(1)}, f32[3,16,32,128]{3,2,1,0:T(8,128)}, u32[]{:S(2)}) copy-start(f32[3,16,32,128]{3,2,1,0:T(8,128)} %load_ref.1) | copy-start | bytes 2359300
  7.5 15.0 %copy-start.6 = (s32[128,128]{1,0:T(8,128)S(1)}, s32[128,128]{1,0:T(8,128)}, u32[]{:S(2)}) copy-start(s32[128,128]{1,0:T(8,128)} %cell_ref.3) | copy-start | bytes 196612
  7.5 15.0 %copy-start.8 = (s32[128,128]{1,0:T(8,128)S(1)}, s32[128,128]{1,0:T(8,128)}, u32[]{:S(2)}) copy-start(s32[128,128]{1,0:T(8,128)} %seg_ref.3) | copy-start | bytes 196612
  22.5 1.0 %copy-start.9 = (f32[16,32,128]{2,1,0:T(8,128)S(1)}, f32[16,32,128]{2,1,0:T(8,128)}, u32[]{:S(2)}) copy-start(f32[16,32,128]{2,1,0:T(8,128)} %stiff_ref.1) | copy-start | bytes 786436

commit v3 on v2

--- a/solution.py
+++ b/solution.py
@@ -7,9 +7,9 @@
 
 LANES = 128
 ROWS = 8
-PIECES = 3
+PIECES = 2
 VMEM = pl.BlockSpec(memory_space=pltpu.VMEM)
-SMEM = pl.BlockSpec(memory_space=pltpu.SMEM)
+HBM = pl.BlockSpec(memory_space=pltpu.HBM)
 
 
 def pieces_of(value):
@@ -25,8 +25,26 @@
     return jnp.take_along_axis(table, index, axis=1, mode="promise_in_bounds")
 
 
+def split_index(index, size):
+    if size & (size - 1):
+        return index // size, index % size
+    return lax.shift_right_logical(index, size.bit_length() - 1), index & (size - 1)
+
+
+def onehot(row, count):
+    kind = jnp.bfloat16 if count <= 256 else jnp.float32
+    ids = lax.broadcasted_iota(jnp.int32, (count, LANES), 0).astype(kind)
+    same = row.astype(kind) == ids
+    return jnp.where(same, jnp.ones_like(ids), jnp.zeros_like(ids)).astype(jnp.bfloat16)
+
+
+def start_all(copies):
+    for copy in copies:
+        copy.start()
+
+
 def gather_rows(rows, index):
-    row, lane = index // LANES, index % LANES
+    row, lane = split_index(index, LANES)
     value = None
     for number, piece in enumerate(rows):
         got = lane_gather(jnp.broadcast_to(piece, index.shape), lane)
@@ -76,25 +94,23 @@
 
     lax.fori_loop(0, blocks // ROWS, prepare, 0, unroll=2)
     acc[...] = jnp.zeros_like(acc)
-    ids = lax.broadcasted_iota(jnp.int32, (segments, LANES), 0)
 
     def add(t, _):
         first = pl.multiple_of(t * ROWS, ROWS)
         left, right = [], []
         for i in range(ROWS):
-            item = terms[pl.ds(pl.multiple_of((first + i) * pad, pad), pad), :].astype(jnp.bfloat16)
+            item = terms[pl.ds(pl.multiple_of((first + i) * pad, pad), pad), :]
             owner = owner_ref[first + i]
             left.append(
                 jnp.concatenate(
                     [jnp.where(owner == o, item, jnp.zeros_like(item)) for o in range(count)], axis=0
-                )
+                ).astype(jnp.bfloat16)
             )
-            segs = seg_ref[pl.ds(first + i, 1), :]
-            right.append(jnp.where(segs == ids, 1.0, 0.0).astype(jnp.bfloat16))
+            right.append(onehot(seg_ref[pl.ds(first + i, 1), :], segments))
         acc[...] += nt_dot(jnp.concatenate(left, axis=1), jnp.concatenate(right, axis=1))
         return 0
 
-    lax.fori_loop(0, blocks // ROWS, add, 0)
+    lax.fori_loop(0, blocks // ROWS, add, 0, unroll=4)
     for o in range(count):
         total = acc[pl.ds(o * pad, pad), :]
         value = total[0:modes]
@@ -104,10 +120,22 @@
 
 
 def exchange_kernel(
-    disp_ref, gap_ref, weight_ref, basis_ref, cell_ref, seg_ref, owner_ref, mult_ref, inv_ref,
-    changes_ref, updated_ref, xhalo_ref, yhalo_ref,
-    terms, acc, partial_ref, face_ref, landed, send1, recv1, send2, recv2, sendx, recvx, sendy, recvy,
+    *refs,
 ):
+    inputs, outputs, held, rest = refs[:12], refs[12:16], refs[16:28], refs[28:]
+    (
+        disp_ref, cell_ref, gap_ref, weight_ref, basis_ref, owner_ref, seg_ref,
+        mult_ref, inv_ref, row_ref, stiff_ref, load_ref,
+    ) = held
+    changes_ref, updated_ref, base_ref, owners_ref = outputs
+    (
+        xhalo_ref, yhalo_ref, load_sem, terms, acc, partial_ref, face_ref, landed, send1, recv1, send2, recv2, sendx, recvx, sendy, recvy,
+    ) = rest
+    loads = [
+        pltpu.make_async_copy(source, target, load_sem.at[i])
+        for i, (source, target) in enumerate(zip(inputs, held))
+    ]
+    start_all(loads)
     count, nb = lax.axis_size("mort"), lax.axis_size("body")
     me, mb = lax.axis_index("mort"), lax.axis_index("body")
     cells_x = disp_ref.shape[1]
@@ -123,6 +151,8 @@
             device_id_type=pl.DeviceIdType.MESH,
         )
     cells_y = disp_ref.shape[2]
+    for copy in loads[:-2]:
+        copy.wait()
     face_ref[0] = disp_ref[:, :, cells_y - 1, :]
     face_ref[1] = disp_ref[:, :, 0, :]
     make_shares(
@@ -203,6 +233,18 @@
 
     for j in range(1, count):
         spread(j).start()
+    owners_ref[...] = jnp.broadcast_to(row_ref[...], (LANES, row_ref.shape[1])).T
+    for copy in loads[-2:]:
+        copy.wait()
+    for make, side, sends, takes in halos:
+
+        @pl.when(takes)
+        def _():
+            make(side).wait_recv()
+
+    for i in range(disp_ref.shape[0]):
+        for x in range(cells_x):
+            base_ref[i, x] = stencil(disp_ref, load_ref, stiff_ref, xhalo_ref, yhalo_ref, i, x)
     for copy in shares:
         copy.wait_send()
     for make, side, sends, takes in halos:
@@ -211,25 +253,44 @@
         def _():
             make(side).wait_send()
 
-        @pl.when(takes)
-        def _():
-            make(side).wait_recv()
-
     for j in range(1, count):
         spread(j).wait_send()
         arrival(j).wait_recv()
 
 
+def stencil(disp_ref, load_ref, stiff_ref, xhalo_ref, yhalo_ref, i, x):
+    _, cells_x, cells_y, nz = disp_ref.shape
+    lane = lax.broadcasted_iota(jnp.int32, (cells_y, nz), 1)
+    row = lax.broadcasted_iota(jnp.int32, (cells_y, nz), 0)
+    here = disp_ref[i, x]
+    low = disp_ref[i, x - 1] if x > 0 else xhalo_ref[0, i]
+    high = disp_ref[i, x + 1] if x < cells_x - 1 else xhalo_ref[1, i]
+    below = jnp.where(row == 0, yhalo_ref[0, i, x : x + 1, :], pltpu.roll(here, 1, 0))
+    above = jnp.where(
+        row == cells_y - 1, yhalo_ref[1, i, x : x + 1, :], pltpu.roll(here, cells_y - 1, 0)
+    )
+    left = jnp.where(lane == 0, 0.0, pltpu.roll(here, 1, 1))
+    right = jnp.where(lane == nz - 1, 0.0, pltpu.roll(here, nz - 1, 1))
+    beside = high + low + above + below + right + left
+    return load_ref[i, x] - ((6.0 + stiff_ref[x]) * here - beside)
+
+
 def residual_kernel(
-    disp_ref, load_ref, stiff_ref, weight_ref, basis_ref, cell_ref, seg_ref, owner_ref,
-    changes_ref, new_ref, xhalo_ref, yhalo_ref,
-    out_ref, updated_ref, loads, owners,
+    base_ref, weight_ref, basis_ref, cell_ref, seg_ref, owners, changes_ref, new_ref,
+    out_hbm, updated_ref, last_ref, loads, spots, out_sems,
 ):
-    parts, cells_x, cells_y, nz = disp_ref.shape
+    parts, cells_x, cells_y, nz = base_ref.shape
     blocks = weight_ref.shape[0]
     count, modes, segments = changes_ref.shape
     updated_ref[...] = new_ref[...]
-    owners[...] = jnp.broadcast_to(owner_ref[...], (LANES, blocks)).T
+
+    def store(i):
+        source = last_ref if i == 2 else base_ref.at[i]
+        return pltpu.make_async_copy(source, out_hbm.at[i], out_sems.at[i])
+
+    for i in range(parts):
+        if i != 2:
+            store(i).start()
 
     def pressures(t, _):
         first = pl.multiple_of(t * ROWS, ROWS)
@@ -249,49 +310,42 @@
             basis = basis_ref[pl.ds(first * modes + k, ROWS, stride=modes), :]
             term = basis * gather_rows(pieces, segs)
             pressure = term if pressure is None else pressure + term
-        loads[rows, :] = weight_ref[rows, :] * pressure
+        for s, piece in enumerate(pieces_of(weight_ref[rows, :] * pressure)):
+            loads[s, rows, :] = piece
+        for s, spot in enumerate(split_index(cell_ref[rows, :], cells_y)):
+            spots[s, rows, :] = spot
         return 0
 
-    lax.fori_loop(0, blocks // ROWS, pressures, 0)
+    lax.fori_loop(0, blocks // ROWS, pressures, 0, unroll=2)
+    lane = lax.broadcasted_iota(jnp.int32, (cells_y, nz), 1)
     xs = lax.broadcasted_iota(jnp.int32, (cells_x, LANES), 0)
-    ys = lax.broadcasted_iota(jnp.int32, (cells_y, LANES), 0)
 
     def spread(t, acc):
         first = t * ROWS
         left, right = [], []
         for i in range(ROWS):
-            cell = cell_ref[pl.ds(first + i, 1), :]
-            at_x, at_y = cell // cells_y, cell % cells_y
-            left.append(jnp.where(at_y == ys, 1.0, 0.0).astype(jnp.bfloat16))
-            value = jnp.where(at_x == xs, loads[pl.ds(first + i, 1), :], 0.0)
-            right.append(jnp.concatenate([p.astype(jnp.bfloat16) for p in pieces_of(value)], axis=0))
+            place = pl.ds(first + i, 1)
+            left.append(onehot(spots[1, place, :], cells_y))
+            same = spots[0, place, :] == xs
+            right.append(
+                jnp.concatenate(
+                    [jnp.where(same, loads[s, place, :], 0.0) for s in range(PIECES)], axis=0
+                ).astype(jnp.bfloat16)
+            )
         return acc + nt_dot(jnp.concatenate(left, axis=1), jnp.concatenate(right, axis=1))
 
     acc = lax.fori_loop(
-        0, blocks // ROWS, spread, jnp.zeros((cells_y, PIECES * cells_x), jnp.float32)
+        0, blocks // ROWS, spread, jnp.zeros((cells_y, PIECES * cells_x), jnp.float32), unroll=4
     )
-    lane = lax.broadcasted_iota(jnp.int32, (cells_y, nz), 1)
-    row = lax.broadcasted_iota(jnp.int32, (cells_y, nz), 0)
     for x in range(cells_x):
-        diagonal = 6.0 + stiff_ref[x]
-        for i in range(parts):
-            here = disp_ref[i, x]
-            low = disp_ref[i, x - 1] if x > 0 else xhalo_ref[0, i]
-            high = disp_ref[i, x + 1] if x < cells_x - 1 else xhalo_ref[1, i]
-            below = jnp.where(row == 0, yhalo_ref[0, i, x : x + 1, :], pltpu.roll(here, 1, 0))
-            above = jnp.where(
-                row == cells_y - 1, yhalo_ref[1, i, x : x + 1, :], pltpu.roll(here, cells_y - 1, 0)
-            )
-            left = jnp.where(lane == 0, 0.0, pltpu.roll(here, 1, 1))
-            right = jnp.where(lane == nz - 1, 0.0, pltpu.roll(here, nz - 1, 1))
-            beside = high + low + above + below + right + left
-            residual = load_ref[i, x] - (diagonal * here - beside)
-            if i == 2:
-                traction = acc[:, x : x + 1]
-                for s in range(1, PIECES):
-                    traction = traction + acc[:, s * cells_x + x : s * cells_x + x + 1]
-                residual = jnp.where(lane == 0, residual + traction, residual)
-            out_ref[i, x] = residual
+        traction = acc[:, x : x + 1]
+        for s in range(1, PIECES):
+            traction = traction + acc[:, s * cells_x + x : s * cells_x + x + 1]
+        residual = base_ref[2, x]
+        last_ref[x] = jnp.where(lane == 0, residual + traction, residual)
+    store(2).start()
+    for i in range(parts):
+        store(i).wait()
 
 
 def body(
@@ -304,21 +358,32 @@
     count = lax.axis_size("mort")
     f32 = jnp.float32
     basis = basis_values.reshape(blocks * modes, points)
-    pad = -(-PIECES * modes // 16) * 16
+    pad = -(-PIECES * modes // ROWS) * ROWS
     shape = jax.ShapeDtypeStruct
     dma = pltpu.SemaphoreType.DMA
-    changes, new, xhalo, yhalo = pl.pallas_call(
+    sources = (
+        displacement, point_cell, initial_gap, weights, basis, block_owner.reshape(blocks),
+        point_segment, multipliers, block_inverse, block_owner.reshape(1, blocks), stiffness,
+        body_load,
+    )
+    changes, new, base, owners = pl.pallas_call(
         exchange_kernel,
         name="exchange",
         out_shape=(
             shape((count, modes, segments), f32),
             shape((modes, segments), f32),
-            shape((2, parts, cells_y, nz), f32),
-            shape((2, parts, cells_x, nz), f32),
+            shape(displacement.shape, f32),
+            shape((blocks, LANES), jnp.int32),
         ),
-        in_specs=[VMEM] * 6 + [SMEM] + [VMEM] * 2,
+        in_specs=[HBM] * len(sources),
         out_specs=(VMEM,) * 4,
         scratch_shapes=[
+            pltpu.SMEM(a.shape, a.dtype) if a.ndim == 1 else pltpu.VMEM(a.shape, a.dtype)
+            for a in sources
+        ]
+        + [pltpu.VMEM((2, parts, cells_y, nz), f32), pltpu.VMEM((2, parts, cells_x, nz), f32)]
+        + [dma((len(sources),))]
+        + [
             pltpu.VMEM((blocks * pad, LANES), f32),
             pltpu.VMEM((count * pad, segments), f32),
             pltpu.VMEM((count, modes, segments), f32),
@@ -330,10 +395,7 @@
         compiler_params=pltpu.CompilerParams(
             vmem_limit_bytes=8 << 20, collective_id=0, has_side_effects=True
         ),
-    )(
-        displacement, initial_gap, weights, basis, point_cell, point_segment,
-        block_owner.reshape(blocks), multipliers, block_inverse,
-    )
+    )(*[pltpu.with_memory_space_constraint(a, pltpu.HBM) for a in sources])
     return pl.pallas_call(
         residual_kernel,
         name="residual",
@@ -342,13 +404,15 @@
             shape(displacement.shape, f32),
             shape((modes, segments), f32),
         ),
-        in_specs=[VMEM] * 12,
-        out_specs=(VMEM, VMEM),
-        scratch_shapes=[pltpu.VMEM((blocks, LANES), f32), pltpu.VMEM((blocks, LANES), jnp.int32)],
-    )(
-        displacement, body_load, stiffness, weights, basis, point_cell, point_segment,
-        block_owner.reshape(1, blocks), changes, new, xhalo, yhalo,
-    )
+        in_specs=[VMEM] * 8,
+        out_specs=(HBM, VMEM),
+        scratch_shapes=[
+            pltpu.VMEM(displacement.shape[1:], f32),
+            pltpu.VMEM((PIECES, blocks, LANES), f32),
+            pltpu.VMEM((2, blocks, LANES), jnp.int32),
+            dma((parts,)),
+        ],
+    )(base, weights, basis, point_cell, point_segment, owners, changes, new)
 
 
 def solution(mesh):

time: 29.9 us -> 18 us (0.60); the launches traced: 29.4 us -> 17.9 us
  local copies, waits for them, and re-layouts: 7.79 us -> 0.02 us
  Pallas kernels: 20.9 us -> 17.1 us
    unnamed x28 -> x8, local copies, waits for them, and re-layouts: 7.79 us -> 0.02 us
    pallas_call x1, Pallas kernels: 5.94 us -> 3.33 us  [body(): pl.pallas_call(residual_kernel, name='residual', compiler_params=pltpu.Co...]
    pallas_call x1, Pallas kernels: 15 us -> 13.8 us  [body(): pl.pallas_call(exchange_kernel, name='exchange', out_shape=(shape((count,...]
where the time goes in v3:
time: 18 us; the launch traced here: 17.9 us
  Pallas kernels  17.1 us (95%)
  between operations  0.71 us (4%)
    pallas_call x1, Pallas kernels, body(): pl.pallas_call(exchange_kernel, name='exchange', out_shape=(shape((count,...  13.8 us
    pallas_call x1, Pallas kernels, body(): pl.pallas_call(residual_kernel, name='residual', compiler_params=pltpu.Co...  3.33 us

profile of v3, /device:TPU:0, one launch (start us, length us, event | category | flops | bytes accessed | tf_op | source)
XLA Modules:
  0.0 17.9 jit_solution(11316995369413179096)
XLA Ops:
  0.6 0.0 copy-start
  0.6 0.0 copy-start.1
  0.7 0.0 copy-start.2
  0.7 0.0 copy-start.3
  0.7 13.8 %exchange.1 = (f32[8,4,256]{2,1,0:T(4,128)S(1)}, f32[4,256]{1,0:T(4,128)S(1)}, f32[3,16,32,128]{3,2,1,0:T(8,128)S(1)}, s32[128,128]{1,0:T(8,128)S(1)}) custom-call(f32[3,16,32,128]{3,2,1,0:T(8,128)} %refs_0_.1, s32[128,128]{1,0:T(8,128)} %cell_ref.1, f32[128,128]{1,0:T(8,128)} %refs_2_.1, f32[128,128]{1,0:T(8,128)} %weight_ref.1, f32[512,128]{1,0:T(8,128)} %bitcast.3, ...), custom_call_target="tpu_custom_call" | custom-call | tf_op jit(solution)/shard_map/exchange/pallas_call | solution.py:369
  14.5 0.0 copy-done
  14.5 0.0 copy-done.1
  14.5 0.0 copy-done.2
  14.5 0.0 copy-done.3
  14.5 3.3 %residual.1 = (f32[3,16,32,128]{3,2,1,0:T(8,128)}, f32[4,256]{1,0:T(4,128)}) custom-call(f32[3,16,32,128]{3,2,1,0:T(8,128)S(1)} %get-tuple-element.6.base_ref, f32[128,128]{1,0:T(8,128)S(1)} %copy-done.2, f32[512,128]{1,0:T(8,128)S(1)} %bitcast.4, s32[128,128]{1,0:T(8,128)S(1)} %copy-done.1, s32[128,128]{1,0:T(8,128)S(1)} %copy-done.3, ...), custom_call_target="tpu_custom_call" | custom-call | tf_op jit(solution)/shard_map/residual/pallas_call | solution.py:399
Async XLA Ops:
  0.6 13.9 %copy-start = (f32[128,4,128]{2,1,0:T(4,128)S(1)}, f32[128,4,128]{2,1,0:T(4,128)}, u32[]{:S(2)}) copy-start(f32[128,4,128]{2,1,0:T(4,128)} %param.16) | copy-start | bytes 786436
  0.6 13.9 %copy-start.1 = (s32[128,128]{1,0:T(8,128)S(1)}, s32[128,128]{1,0:T(8,128)}, u32[]{:S(2)}) copy-start(s32[128,128]{1,0:T(8,128)} %cell_ref.1) | copy-start | bytes 196612
  0.7 13.9 %copy-start.2 = (f32[128,128]{1,0:T(8,128)S(1)}, f32[128,128]{1,0:T(8,128)}, u32[]{:S(2)}) copy-start(f32[128,128]{1,0:T(8,128)} %weight_ref.1) | copy-start | bytes 196612
  0.7 13.9 %copy-start.3 = (s32[128,128]{1,0:T(8,128)S(1)}, s32[128,128]{1,0:T(8,128)}, u32[]{:S(2)}) copy-start(s32[128,128]{1,0:T(8,128)} %seg_ref.1) | copy-start | bytes 196612
